TPU v7x, 512 devices: a whole 4x8x8 slice. The times are simulated.
512 devices in a mesh: pipe: 32 (over z_hi, y), dp: 16 (over x, z_lo, core).
Axes of the slice: x: 4, y: 8, z: 8 (z_hi: 4, z_lo: 2; z = z_hi * 2 + z_lo), core: 2. Of those that a mesh axis runs over, the one named last changes fastest.
Arguments:
- section_inputs: bfloat16 [32, 3072, 6144], P('pipe', 'dp'), may hold values from -6 to 6
- loss_grad: bfloat16 [3072, 6144], P('dp', 'pipe'), may hold values from -6 to 6
- weight_blocks: bfloat16 [32, 48, 128, 128], P('pipe', 'dp'), may hold values from -0.3125 to 0.3125
- left_factor: bfloat16 [32, 6144, 64], P('pipe', 'dp'), may hold values from -0.078125 to 0.078125
- right_factor: bfloat16 [32, 64, 6144], P('pipe', None, 'dp'), may hold values from -0.5 to 0.5
- block_column: int32 [32, 48], P('pipe'), may hold values from 0 to 47, each once within a row
- live_length: int32 [16, 12], P('dp'), may hold values from 1 to 16, 144 in all within a row
Outputs:
- in_grad: bfloat16 [32, 3072, 6144], P('pipe', 'dp')
- grad_blocks: bfloat16 [32, 48, 128, 128], P('pipe', 'dp')
- grad_left: bfloat16 [32, 6144, 64], P('pipe', 'dp')
- grad_right: bfloat16 [32, 64, 6144], P('pipe', None, 'dp')
Inputs may be any that keep to these rules, and one draw needn't show every extreme that they name: `block_column`: each section's row is a permutation of 0 to 47. `live_length`: each row sums to 144 live tokens.
All inputs are finite; a program needn't handle non-finite values.
Results may differ from a plain program's by a relative error of at most 0.035.
Values may be sent and summed in bfloat16 or wider, within the bound.
A program may use at most 64 MiB of HBM per device.

v0:
```python
import math
import jax
import jax.numpy as jnp
from jax import lax
from jax.sharding import PartitionSpec as P


def shifted(shard, axis, by):
    count = lax.axis_size(axis)
    pairs = [(i, i + by) for i in range(count) if 0 <= i + by < count]
    return lax.ppermute(shard, axis, pairs)


def slope_of(values):
    cumulative = 0.5 * (1.0 + jax.scipy.special.erf(values * (1.0 / math.sqrt(2.0))))
    density = jnp.exp(-0.5 * values * values) * (1.0 / math.sqrt(2.0 * math.pi))
    return cumulative + values * density


def inverse_of(columns):
    number = columns.shape[0]
    ladder = jnp.arange(number, dtype=jnp.int32)
    matches = (columns[:, None] == ladder[None, :]).astype(jnp.int32)
    return jnp.sum(matches * ladder[:, None], axis=0)


def section_rows(inputs, incoming, blocks, left_whole, right_whole, columns, inverse):
    row_count, features = inputs.shape
    number, block_size = (blocks.shape[0], blocks.shape[1])
    split_in = inputs.reshape(row_count, number, block_size)
    sparse = jnp.einsum("tnb,nbc->tnc", split_in, blocks, preferred_element_type=jnp.float32)
    sparse = jnp.take(sparse, inverse, axis=1).reshape(row_count, features)
    lowered = jnp.dot(inputs, left_whole, preferred_element_type=jnp.float32).astype(jnp.bfloat16)
    preactivation = sparse + jnp.dot(lowered, right_whole, preferred_element_type=jnp.float32)
    delta_grad = (incoming.astype(jnp.float32) * slope_of(preactivation)).astype(jnp.bfloat16)
    delta_split = jnp.take(delta_grad.reshape(row_count, number, block_size), columns, axis=1)
    back_sparse = jnp.einsum(
        "tnc,nbc->tnb", delta_split, blocks, preferred_element_type=jnp.float32
    ).reshape(row_count, features)
    reduced = jnp.einsum(
        "td,rd->tr", delta_grad, right_whole, preferred_element_type=jnp.float32
    ).astype(jnp.bfloat16)
    back_low = jnp.einsum("tr,dr->td", reduced, left_whole, preferred_element_type=jnp.float32)
    outgoing = (incoming.astype(jnp.float32) + back_sparse + back_low).astype(jnp.bfloat16)
    return (outgoing, delta_split, lowered, reduced)


def weight_terms(inputs, delta_split, lowered, reduced):
    row_count, features = inputs.shape
    number, block_size = (delta_split.shape[1], delta_split.shape[2])
    split_in = inputs.reshape(row_count, number, block_size)
    grad_blocks = jnp.einsum(
        "tnb,tnc->nbc", split_in, delta_split, preferred_element_type=jnp.float32
    )
    grad_left = jnp.einsum("td,tr->dr", inputs, reduced, preferred_element_type=jnp.float32)
    grad_mixed = jnp.einsum("tr,tnc->rnc", lowered, delta_split, preferred_element_type=jnp.float32)
    return (grad_blocks, grad_left, grad_mixed)


def replace_rows(buffer, fresh, start, active):
    older = lax.dynamic_slice_in_dim(buffer, start, fresh.shape[0], 0)
    return lax.dynamic_update_slice_in_dim(buffer, jnp.where(active, fresh, older), start, 0)


def body(
    section_inputs, loss_grad, weight_blocks, left_factor, right_factor, block_column, live_length
):
    inputs = section_inputs[0]
    blocks, left_whole, right_whole = (
        lax.all_gather(weight_blocks[0], "dp", axis=0, tiled=True),
        lax.all_gather(left_factor[0], "dp", axis=0, tiled=True),
        lax.all_gather(right_factor[0], "dp", axis=1, tiled=True),
    )
    head = lax.all_gather(loss_grad, "pipe", axis=1, tiled=True)
    columns = block_column[0]
    inverse = inverse_of(columns)
    sections = lax.axis_size("pipe")
    section = lax.axis_index("pipe")
    token_count, features = inputs.shape
    micro_count = live_length.shape[1]
    micro_rows = token_count // micro_count
    number, block_size = (blocks.shape[0], blocks.shape[1])
    rank_width = left_whole.shape[1]
    positions = jnp.arange(token_count, dtype=jnp.int32)
    owners = (positions // micro_rows)[:, None] == jnp.arange(micro_count, dtype=jnp.int32)[None, :]
    limits = jnp.sum(jnp.where(owners, live_length[0][None, :], 0), axis=1)
    live_rows = positions % micro_rows < limits
    seeded = jnp.where(live_rows[:, None], head, jnp.zeros_like(head))
    work_count = inputs.shape[0]
    turns = micro_count + sections - 1
    stored = (
        jnp.zeros((work_count, number, block_size), jnp.bfloat16),
        jnp.zeros((work_count, rank_width), jnp.bfloat16),
        jnp.zeros((work_count, rank_width), jnp.bfloat16),
    )

    def compute(upstream, rows_in):
        return section_rows(rows_in, upstream, blocks, left_whole, right_whole, columns, inverse)

    def skipped(upstream, rows_in):
        return (
            jnp.zeros_like(upstream),
            jnp.zeros((micro_rows, number, block_size), jnp.bfloat16),
            jnp.zeros((micro_rows, rank_width), jnp.bfloat16),
            jnp.zeros((micro_rows, rank_width), jnp.bfloat16),
        )

    def turn(index, carry):
        incoming, grads_out, saved = carry
        micro = index - (sections - 1 - section)
        active = (micro >= 0) & (micro < micro_count)
        start = jnp.clip(micro, 0, micro_count - 1) * micro_rows
        rows_in = lax.dynamic_slice_in_dim(inputs, start, micro_rows, 0)
        from_head = lax.dynamic_slice_in_dim(seeded, start, micro_rows, 0)
        upstream = jnp.where(section == sections - 1, from_head, incoming)
        outgoing, delta_split, lowered, reduced = lax.cond(
            active, compute, skipped, upstream, rows_in
        )
        grads_out = replace_rows(grads_out, outgoing, start, active)
        saved = (
            replace_rows(saved[0], delta_split, start, active),
            replace_rows(saved[1], lowered, start, active),
            replace_rows(saved[2], reduced, start, active),
        )
        passed = shifted(outgoing, "pipe", -1)
        return (passed, grads_out, saved)

    start_grad = jnp.zeros((micro_rows, features), jnp.bfloat16)
    unused, work_grad, saved = lax.fori_loop(
        0, turns, turn, (start_grad, jnp.zeros_like(inputs), stored)
    )
    grad_blocks, grad_left, grad_mixed = weight_terms(inputs, saved[0], saved[1], saved[2])
    grad_right = jnp.take(grad_mixed, inverse, axis=1).reshape(rank_width, features)
    sum_blocks, sum_left, sum_right = (
        lax.psum_scatter(
            grad_blocks.astype(jnp.bfloat16), "dp", scatter_dimension=0, tiled=True
        ).astype(jnp.float32),
        lax.psum_scatter(
            grad_left.astype(jnp.bfloat16), "dp", scatter_dimension=0, tiled=True
        ).astype(jnp.float32),
        lax.psum_scatter(
            grad_right.astype(jnp.bfloat16), "dp", scatter_dimension=1, tiled=True
        ).astype(jnp.float32),
    )
    return (
        work_grad[None],
        sum_blocks.astype(jnp.bfloat16)[None],
        sum_left.astype(jnp.bfloat16)[None],
        sum_right.astype(jnp.bfloat16)[None],
    )


def solution(mesh):
    in_specs = (
        P("pipe", "dp", None),
        P("dp", "pipe"),
        P("pipe", "dp", None, None),
        P("pipe", "dp", None),
        P("pipe", None, "dp"),
        P("pipe", None),
        P("dp", None),
    )
    out_specs = (
        P("pipe", "dp", None),
        P("pipe", "dp", None, None),
        P("pipe", "dp", None),
        P("pipe", None, "dp"),
    )
    return jax.shard_map(body, mesh=mesh, in_specs=in_specs, out_specs=out_specs, check_vma=False)
```

profile of v0, /device:TPU:8, one launch (start us, length us, event | category | flops | bytes accessed | tf_op | source)
XLA Modules:
  0.0 1399.3 jit_solution(17293354459489336557)
XLA Ops:
  15.0 29.2 %all-gather.1 = bf16[1,6144,64]{2,1,0:T(8,128)(2,1)S(1)} all-gather(bf16[1,384,64]{2,1,0:T(8,128)(2,1)S(1)} %copy.44), channel_id=3, replica_groups=mesh['pipe'=32,'dp'=16] {'dp'}, dimensions={1}, use_global_device_ids=true | all-gather | bytes 835584 | tf_op jit(solution)/shard_map/all_gather | solution.py:71
  44.2 23.6 %all-gather.2 = bf16[1,64,6144]{2,1,0:T(8,128)(2,1)} all-gather(bf16[1,64,384]{2,1,0:T(8,128)(2,1)} %param.15), channel_id=4, replica_groups=mesh['pipe'=32,'dp'=16] {'dp'}, dimensions={2}, use_global_device_ids=true | all-gather | bytes 835584 | tf_op jit(solution)/shard_map/all_gather | solution.py:72
  67.8 41.7 %all-gather.6.cloned.1.call-done = bf16[192,6144]{0,1:T(8,128)(2,1)} async-done(((bf16[192,192]{0,1:T(8,128)(2,1)}), bf16[192,6144]{0,1:T(8,128)(2,1)}) %all-gather.6.cloned.1.call-update) | async-done | bytes 2359312 | tf_op jit(solution)/shard_map/all_gather | solution.py:74
  109.5 3.8 broadcast_select_fusion
  113.3 4.6 copy.46
  117.9 28.8 %all-gather.8.cloned.1.call-done = bf16[1,48,128,128]{3,2,0,1:T(8,128)(2,1)} async-done(((bf16[1,3,128,128]{3,2,0,1:T(8,128)(2,1)}), bf16[1,48,128,128]{3,2,0,1:T(8,128)(2,1)}) %all-gather.8.cloned.1.call-update) | async-done | bytes 1572880 | tf_op jit(solution)/shard_map/all_gather | solution.py:70
  152.3 1034.6 %while.23 = (s32[]{:T(128)}, bf16[16,6144]{1,0:T(8,128)(2,1)}, bf16[192,6144]{1,0:T(8,128)(2,1)}, bf16[192,48,128]{2,0,1:T(8,128)(2,1)}, bf16[192,64]{1,0:T(8,12...) while((s32[]{:T(128)}, bf16[16,6144]{1,0:T(8,128)(2,1)}, ...), condition=%wide.region_5.6_spmd, body=%wide.region_2.5_spmd.sunk | while | flops 102833008 | bytes 20126928 | solution.py:129
  154.3 2.4 collective-permute-start
  166.1 2.4 collective-permute-start
  177.1 2.4 collective-permute-start
  206.0 2.4 collective-permute-done
  217.7 2.4 collective-permute-done
  229.3 2.4 collective-permute-done
  241.0 2.4 collective-permute-done
  252.7 6.2 collective-permute-done
  268.1 5.0 collective-permute-done
  282.4 3.5 collective-permute-done
  295.2 5.9 collective-permute-done
  310.4 6.2 collective-permute-done
  325.9 5.6 collective-permute-done
  340.9 5.2 collective-permute-done
  355.4 5.2 collective-permute-done
  369.8 3.7 collective-permute-done
  382.9 3.9 collective-permute-done
  396.0 4.2 collective-permute-done
  409.5 4.6 collective-permute-done
  423.4 6.6 collective-permute-done
  439.3 8.9 collective-permute-done
  457.5 7.8 collective-permute-done
  474.6 5.2 collective-permute-done
  489.1 3.7 collective-permute-done
  502.1 5.1 collective-permute-done
  516.5 3.8 collective-permute-done
  529.6 2.4 collective-permute-done
  541.3 2.4 collective-permute-done
  553.0 272.2 %collective-permute-done = bf16[16,6144]{1,0:T(8,128)(2,1)S(1)} collective-permute-done((bf16[16,6144]{1,0:T(8,128)(2,1)}, bf16[16,6144]{1,0:T(8,128)(2,1)S(1)}, u32[]{:S(2)}, u32[]{:S(2)}) %collective-permute-start) | collective-permute-done | bytes 196640 | tf_op jit(solution)/shard_map/while/body/eval_jaxpr/ppermute | solution.py:11
  825.8 14.4 %conditional.2 = (bf16[16,6144]{1,0:T(8,128)(2,1)}, bf16[16,48,128]{2,0,1:T(8,128)(2,1)}, bf16[16,64]{1,0:T(8,128)(2,1)S(1)}, bf16[16,64]{1,0:T(8,128)(2,1)}) conditional(s32[]{:T(128)} %convert_element_type.80, () %tuple.65, (pred[]{:T(512)}, bf16[192,6144]{1,0:T(8,128)(2,1)}, s32[]{:T(128)}, bf16[16,6144]{1,0:T(8,128)(2,1)}, s32[48]{0:T(128)}, ...), branch_computations={%region_3.3_spmd, %region_4.4_spmd} | conditional | flops 102634336 | bytes 17349906 | solution.py:116
  847.1 5.8 collective-permute-done
  853.6 14.4 %conditional.2 = (bf16[16,6144]{1,0:T(8,128)(2,1)}, bf16[16,48,128]{2,0,1:T(8,128)(2,1)}, bf16[16,64]{1,0:T(8,128)(2,1)S(1)}, bf16[16,64]{1,0:T(8,128)(2,1)}) conditional(s32[]{:T(128)} %convert_element_type.80, () %tuple.65, (pred[]{:T(512)}, bf16[192,6144]{1,0:T(8,128)(2,1)}, s32[]{:T(128)}, bf16[16,6144]{1,0:T(8,128)(2,1)}, s32[48]{0:T(128)}, ...), branch_computations={%region_3.3_spmd, %region_4.4_spmd} | conditional | flops 102634336 | bytes 17349906 | solution.py:116
  874.8 6.3 collective-permute-done
  881.8 14.4 %conditional.2 = (bf16[16,6144]{1,0:T(8,128)(2,1)}, bf16[16,48,128]{2,0,1:T(8,128)(2,1)}, bf16[16,64]{1,0:T(8,128)(2,1)S(1)}, bf16[16,64]{1,0:T(8,128)(2,1)}) conditional(s32[]{:T(128)} %convert_element_type.80, () %tuple.65, (pred[]{:T(512)}, bf16[192,6144]{1,0:T(8,128)(2,1)}, s32[]{:T(128)}, bf16[16,6144]{1,0:T(8,128)(2,1)}, s32[48]{0:T(128)}, ...), branch_computations={%region_3.3_spmd, %region_4.4_spmd} | conditional | flops 102634336 | bytes 17349906 | solution.py:116
  903.0 8.3 collective-permute-done
  912.0 14.4 %conditional.2 = (bf16[16,6144]{1,0:T(8,128)(2,1)}, bf16[16,48,128]{2,0,1:T(8,128)(2,1)}, bf16[16,64]{1,0:T(8,128)(2,1)S(1)}, bf16[16,64]{1,0:T(8,128)(2,1)}) conditional(s32[]{:T(128)} %convert_element_type.80, () %tuple.65, (pred[]{:T(512)}, bf16[192,6144]{1,0:T(8,128)(2,1)}, s32[]{:T(128)}, bf16[16,6144]{1,0:T(8,128)(2,1)}, s32[48]{0:T(128)}, ...), branch_computations={%region_3.3_spmd, %region_4.4_spmd} | conditional | flops 102634336 | bytes 17349906 | solution.py:116
  933.2 8.3 collective-permute-done
  942.2 14.4 %conditional.2 = (bf16[16,6144]{1,0:T(8,128)(2,1)}, bf16[16,48,128]{2,0,1:T(8,128)(2,1)}, bf16[16,64]{1,0:T(8,128)(2,1)S(1)}, bf16[16,64]{1,0:T(8,128)(2,1)}) conditional(s32[]{:T(128)} %convert_element_type.80, () %tuple.65, (pred[]{:T(512)}, bf16[192,6144]{1,0:T(8,128)(2,1)}, s32[]{:T(128)}, bf16[16,6144]{1,0:T(8,128)(2,1)}, s32[48]{0:T(128)}, ...), branch_computations={%region_3.3_spmd, %region_4.4_spmd} | conditional | flops 102634336 | bytes 17349906 | solution.py:116
  963.4 6.8 collective-permute-done
  970.9 14.4 %conditional.2 = (bf16[16,6144]{1,0:T(8,128)(2,1)}, bf16[16,48,128]{2,0,1:T(8,128)(2,1)}, bf16[16,64]{1,0:T(8,128)(2,1)S(1)}, bf16[16,64]{1,0:T(8,128)(2,1)}) conditional(s32[]{:T(128)} %convert_element_type.80, () %tuple.65, (pred[]{:T(512)}, bf16[192,6144]{1,0:T(8,128)(2,1)}, s32[]{:T(128)}, bf16[16,6144]{1,0:T(8,128)(2,1)}, s32[48]{0:T(128)}, ...), branch_computations={%region_3.3_spmd, %region_4.4_spmd} | conditional | flops 102634336 | bytes 17349906 | solution.py:116
  992.1 4.0 collective-permute-done
  996.8 14.4 %conditional.2 = (bf16[16,6144]{1,0:T(8,128)(2,1)}, bf16[16,48,128]{2,0,1:T(8,128)(2,1)}, bf16[16,64]{1,0:T(8,128)(2,1)S(1)}, bf16[16,64]{1,0:T(8,128)(2,1)}) conditional(s32[]{:T(128)} %convert_element_type.80, () %tuple.65, (pred[]{:T(512)}, bf16[192,6144]{1,0:T(8,128)(2,1)}, s32[]{:T(128)}, bf16[16,6144]{1,0:T(8,128)(2,1)}, s32[48]{0:T(128)}, ...), branch_computations={%region_3.3_spmd, %region_4.4_spmd} | conditional | flops 102634336 | bytes 17349906 | solution.py:116
  1018.0 5.3 collective-permute-done
  1024.0 14.4 %conditional.2 = (bf16[16,6144]{1,0:T(8,128)(2,1)}, bf16[16,48,128]{2,0,1:T(8,128)(2,1)}, bf16[16,64]{1,0:T(8,128)(2,1)S(1)}, bf16[16,64]{1,0:T(8,128)(2,1)}) conditional(s32[]{:T(128)} %convert_element_type.80, () %tuple.65, (pred[]{:T(512)}, bf16[192,6144]{1,0:T(8,128)(2,1)}, s32[]{:T(128)}, bf16[16,6144]{1,0:T(8,128)(2,1)}, s32[48]{0:T(128)}, ...), branch_computations={%region_3.3_spmd, %region_4.4_spmd} | conditional | flops 102634336 | bytes 17349906 | solution.py:116
  1045.2 5.5 collective-permute-done
  1051.4 14.4 %conditional.2 = (bf16[16,6144]{1,0:T(8,128)(2,1)}, bf16[16,48,128]{2,0,1:T(8,128)(2,1)}, bf16[16,64]{1,0:T(8,128)(2,1)S(1)}, bf16[16,64]{1,0:T(8,128)(2,1)}) conditional(s32[]{:T(128)} %convert_element_type.80, () %tuple.65, (pred[]{:T(512)}, bf16[192,6144]{1,0:T(8,128)(2,1)}, s32[]{:T(128)}, bf16[16,6144]{1,0:T(8,128)(2,1)}, s32[48]{0:T(128)}, ...), branch_computations={%region_3.3_spmd, %region_4.4_spmd} | conditional | flops 102634336 | bytes 17349906 | solution.py:116
  1072.6 7.1 collective-permute-done
  1080.4 14.4 %conditional.2 = (bf16[16,6144]{1,0:T(8,128)(2,1)}, bf16[16,48,128]{2,0,1:T(8,128)(2,1)}, bf16[16,64]{1,0:T(8,128)(2,1)S(1)}, bf16[16,64]{1,0:T(8,128)(2,1)}) conditional(s32[]{:T(128)} %convert_element_type.80, () %tuple.65, (pred[]{:T(512)}, bf16[192,6144]{1,0:T(8,128)(2,1)}, s32[]{:T(128)}, bf16[16,6144]{1,0:T(8,128)(2,1)}, s32[48]{0:T(128)}, ...), branch_computations={%region_3.3_spmd, %region_4.4_spmd} | conditional | flops 102634336 | bytes 17349906 | solution.py:116
  1101.6 13.1 collective-permute-done
  1115.3 14.4 %conditional.2 = (bf16[16,6144]{1,0:T(8,128)(2,1)}, bf16[16,48,128]{2,0,1:T(8,128)(2,1)}, bf16[16,64]{1,0:T(8,128)(2,1)S(1)}, bf16[16,64]{1,0:T(8,128)(2,1)}) conditional(s32[]{:T(128)} %convert_element_type.80, () %tuple.65, (pred[]{:T(512)}, bf16[192,6144]{1,0:T(8,128)(2,1)}, s32[]{:T(128)}, bf16[16,6144]{1,0:T(8,128)(2,1)}, s32[48]{0:T(128)}, ...), branch_computations={%region_3.3_spmd, %region_4.4_spmd} | conditional | flops 102634336 | bytes 17349906 | solution.py:116
  1136.5 5.4 collective-permute-done
  1142.6 14.3 %conditional.2 = (bf16[16,6144]{1,0:T(8,128)(2,1)}, bf16[16,48,128]{2,0,1:T(8,128)(2,1)}, bf16[16,64]{1,0:T(8,128)(2,1)S(1)}, bf16[16,64]{1,0:T(8,128)(2,1)}) conditional(s32[]{:T(128)} %convert_element_type.80, () %tuple.65, (pred[]{:T(512)}, bf16[192,6144]{1,0:T(8,128)(2,1)}, s32[]{:T(128)}, bf16[16,6144]{1,0:T(8,128)(2,1)}, s32[48]{0:T(128)}, ...), branch_computations={%region_3.3_spmd, %region_4.4_spmd} | conditional | flops 102634336 | bytes 17349906 | solution.py:116
  1167.4 14.2 %collective-permute-start = (bf16[16,6144]{1,0:T(8,128)(2,1)}, bf16[16,6144]{1,0:T(8,128)(2,1)S(1)}, u32[]{:S(2)}, u32[]{:S(2)}) collective-permute-start(bf16[16,6144]{1,0:T(8,128)(2,1)} %get-tuple-element.597), channel_id=1, source_target_pairs={{16,0},{32,16},{48,32},{64,48},{80,64},{96,80},{112,96},{128,112},... | collective-permute-start | bytes 589832 | tf_op jit(solution)/shard_map/while/body/eval_jaxpr/ppermute | solution.py:11
  1195.8 2.3 copy.62
  1200.5 51.9 %reduce-scatter.12.cloned.1.call-done = bf16[384,64]{1,0:T(8,128)(2,1)} async-done(((bf16[6144,64]{1,0:T(8,128)(2,1)}), bf16[384,64]{1,0:T(8,128)(2,1)}) %reduce-scatter.12.cloned.1.call-update) | async-done | bytes 49168
  1254.0 67.6 %reduce-scatter.10.cloned.1.call-done = bf16[384,64]{1,0:T(8,128)(2,1)} async-done(((bf16[6144,64]{1,0:T(8,128)(2,1)}), bf16[384,64]{1,0:T(8,128)(2,1)}) %reduce-scatter.10.cloned.1.call-update) | async-done | bytes 49168
  1323.2 67.9 %reduce-scatter.8.cloned.1.call-done = bf16[3,128,128]{1,2,0:T(8,128)(2,1)} async-done(((bf16[48,128,128]{1,2,0:T(8,128)(2,1)}), bf16[3,128,128]{1,2,0:T(8,128)(2,1)}) %reduce-scatter.8.cloned.1.call-update) | async-done | bytes 98320 | tf_op jit(solution)/shard_map/reduce_scatter | solution.py:135
  (782 shorter events, 640.7 us)
Async XLA Ops:
  7.2 102.3 %all-gather.6.cloned.1.call-start = ((), (), s32[]{:S(2)}) async-start(), calls=%async_computation.3 | async-start | bytes 3244032 | tf_op jit(solution)/shard_map/all_gather | solution.py:74
  8.9 137.8 %all-gather.8.cloned.1.call-start = ((), (), s32[]{:S(2)}) async-start(), calls=%async_computation.5 | async-start | bytes 1671168 | tf_op jit(solution)/shard_map/all_gather | solution.py:70
  9.6 1242.8 %reduce-scatter.12.cloned.1.call-start = ((), (), s32[]{:S(2)}) async-start(), calls=%async_computation.7 | async-start | bytes 1671168
  146.7 5.6 copy-start
  154.3 9.1 collective-permute-start
  166.1 8.3 collective-permute-start
  177.1 8.4 collective-permute-start
  188.2 8.5 collective-permute-start
  199.4 9.0 collective-permute-start
  211.1 9.0 collective-permute-start
  222.7 9.0 collective-permute-start
  234.4 9.0 collective-permute-start
  246.1 12.7 collective-permute-start
  261.5 11.6 collective-permute-start
  275.8 10.1 collective-permute-start
  288.6 12.5 collective-permute-start
  303.8 12.8 collective-permute-start
  319.3 12.2 collective-permute-start
  334.3 11.8 collective-permute-start
  348.8 11.8 collective-permute-start
  363.3 10.3 collective-permute-start
  376.3 10.5 collective-permute-start
  389.5 10.8 collective-permute-start
  402.9 11.2 collective-permute-start
  416.8 13.2 collective-permute-start
  432.7 15.5 %collective-permute-start = (bf16[16,6144]{1,0:T(8,128)(2,1)}, bf16[16,6144]{1,0:T(8,128)(2,1)S(1)}, u32[]{:S(2)}, u32[]{:S(2)}) collective-permute-start(bf16[16,6144]{1,0:T(8,128)(2,1)} %get-tuple-element.597), channel_id=1, source_target_pairs={{16,0},{32,16},{48,32},{64,48},{80,64},{96,80},{112,96},{128,112},... | collective-permute-start | bytes 589832 | tf_op jit(solution)/shard_map/while/body/eval_jaxpr/ppermute | solution.py:11
  450.9 14.4 %collective-permute-start = (bf16[16,6144]{1,0:T(8,128)(2,1)}, bf16[16,6144]{1,0:T(8,128)(2,1)S(1)}, u32[]{:S(2)}, u32[]{:S(2)}) collective-permute-start(bf16[16,6144]{1,0:T(8,128)(2,1)} %get-tuple-element.597), channel_id=1, source_target_pairs={{16,0},{32,16},{48,32},{64,48},{80,64},{96,80},{112,96},{128,112},... | collective-permute-start | bytes 589832 | tf_op jit(solution)/shard_map/while/body/eval_jaxpr/ppermute | solution.py:11
  468.0 11.8 collective-permute-start
  482.5 10.3 collective-permute-start
  495.6 11.7 collective-permute-start
  509.9 10.4 collective-permute-start
  523.0 9.0 collective-permute-start
  534.7 9.0 collective-permute-start
  546.4 278.8 %collective-permute-start = (bf16[16,6144]{1,0:T(8,128)(2,1)}, bf16[16,6144]{1,0:T(8,128)(2,1)S(1)}, u32[]{:S(2)}, u32[]{:S(2)}) collective-permute-start(bf16[16,6144]{1,0:T(8,128)(2,1)} %get-tuple-element.597), channel_id=1, source_target_pairs={{16,0},{32,16},{48,32},{64,48},{80,64},{96,80},{112,96},{128,112},... | collective-permute-start | bytes 589832 | tf_op jit(solution)/shard_map/while/body/eval_jaxpr/ppermute | solution.py:11
  830.6 6.5 copy-start.7
  834.5 3.6 copy-start.5
  840.3 12.6 collective-permute-start
  858.4 6.5 copy-start.7
  862.2 3.6 copy-start.5
  868.0 13.1 collective-permute-start
  886.6 6.5 copy-start.7
  896.2 15.1 %collective-permute-start = (bf16[16,6144]{1,0:T(8,128)(2,1)}, bf16[16,6144]{1,0:T(8,128)(2,1)S(1)}, u32[]{:S(2)}, u32[]{:S(2)}) collective-permute-start(bf16[16,6144]{1,0:T(8,128)(2,1)} %get-tuple-element.597), channel_id=1, source_target_pairs={{16,0},{32,16},{48,32},{64,48},{80,64},{96,80},{112,96},{128,112},... | collective-permute-start | bytes 589832 | tf_op jit(solution)/shard_map/while/body/eval_jaxpr/ppermute | solution.py:11
  916.8 6.5 copy-start.7
  926.4 15.1 %collective-permute-start = (bf16[16,6144]{1,0:T(8,128)(2,1)}, bf16[16,6144]{1,0:T(8,128)(2,1)S(1)}, u32[]{:S(2)}, u32[]{:S(2)}) collective-permute-start(bf16[16,6144]{1,0:T(8,128)(2,1)} %get-tuple-element.597), channel_id=1, source_target_pairs={{16,0},{32,16},{48,32},{64,48},{80,64},{96,80},{112,96},{128,112},... | collective-permute-start | bytes 589832 | tf_op jit(solution)/shard_map/while/body/eval_jaxpr/ppermute | solution.py:11
  947.0 6.5 copy-start.7
  950.8 3.6 copy-start.5
  956.6 13.6 collective-permute-start
  975.7 6.5 copy-start.7
  985.4 10.7 collective-permute-start
  1001.6 6.5 copy-start.7
  1011.2 12.1 collective-permute-start
  1028.8 6.5 copy-start.7
  1038.5 12.2 collective-permute-start
  1056.2 6.5 copy-start.7
  1065.8 13.8 collective-permute-start
  1085.1 6.5 copy-start.7
  1094.8 19.8 %collective-permute-start = (bf16[16,6144]{1,0:T(8,128)(2,1)}, bf16[16,6144]{1,0:T(8,128)(2,1)S(1)}, u32[]{:S(2)}, u32[]{:S(2)}) collective-permute-start(bf16[16,6144]{1,0:T(8,128)(2,1)} %get-tuple-element.597), channel_id=1, source_target_pairs={{16,0},{32,16},{48,32},{64,48},{80,64},{96,80},{112,96},{128,112},... | collective-permute-start | bytes 589832 | tf_op jit(solution)/shard_map/while/body/eval_jaxpr/ppermute | solution.py:11
  1120.1 6.5 copy-start.7
  1129.7 12.2 collective-permute-start
  1147.3 6.5 copy-start.7
  1156.9 7.8 collective-permute-start
  1167.4 18.9 %collective-permute-start = (bf16[16,6144]{1,0:T(8,128)(2,1)}, bf16[16,6144]{1,0:T(8,128)(2,1)S(1)}, u32[]{:S(2)}, u32[]{:S(2)}) collective-permute-start(bf16[16,6144]{1,0:T(8,128)(2,1)} %get-tuple-element.597), channel_id=1, source_target_pairs={{16,0},{32,16},{48,32},{64,48},{80,64},{96,80},{112,96},{128,112},... | collective-permute-start | bytes 589832 | tf_op jit(solution)/shard_map/while/body/eval_jaxpr/ppermute | solution.py:11
  1191.8 129.8 %reduce-scatter.10.cloned.1.call-start = ((), (), s32[]{:S(2)}) async-start(), calls=%async_computation.6 | async-start | bytes 1671168
  1195.7 195.4 %reduce-scatter.8.cloned.1.call-start = ((), (), s32[]{:S(2)}) async-start(), calls=%async_computation.4 | async-start | bytes 1671168 | tf_op jit(solution)/shard_map/reduce_scatter | solution.py:135
  (103 other events, 168.1 us)
Sparse Core Ops, SparseCore 0:
  11.7 97.7 all-gather.5
  111.6 35.0 all-gather.7
  1191.9 60.4 reduce-scatter.11
  1255.1 66.4 reduce-scatter.9
  1324.3 66.7 reduce-scatter.7
where the time goes:
time: 1410 us; the launch traced here: 1400 us
  waiting for transfers between devices  729 us (52%)
  other arithmetic  237 us (17%)
  local copies, waits for them, and re-layouts  150 us (11%)
  matrix products  120 us (9%)
  starting transfers between devices  96.1 us (7%)
  blocking collectives  52.8 us (4%)
    ppermute x43, waiting for transfers between devices, shifted(): return lax.ppermute(shard, axis, pairs)  470 us
    dynamic_update_slice x129, other arithmetic, replace_rows(): lax.dynamic_update_slice_in_dim(buffer, jnp.where(active, fresh, older),...  203 us
    unnamed x7, waiting for transfers between devices  120 us
    ppermute x43, starting transfers between devices, shifted(): return lax.ppermute(shard, axis, pairs)  95.9 us
    reduce_scatter x1, waiting for transfers between devices, body(): lax.psum_scatter(grad_blocks.astype(jnp.bfloat16), 'dp', scatter_dimensio...  67.9 us
    another operation x128, local copies, waits for them, and re-layouts  65.9 us
    all_gather x1, waiting for transfers between devices, body(): head = lax.all_gather(loss_grad, 'pipe', axis=1, tiled=True)  41.7 us
    while x86, local copies, waits for them, and re-layouts  29.6 us
  transfers between devices with their start and end apart: 48, of which 47 were waited for; matrix products, arithmetic and copies ran while one was open for 16% of the time, Pallas kernels for 0%

commit v1 on v0

--- a/solution.py
+++ b/solution.py
@@ -3,6 +3,13 @@
 import jax.numpy as jnp
 from jax import lax
 from jax.sharding import PartitionSpec as P
+
+
+def gather_over(block, name, along):
+    size = lax.axis_size(name)
+    blocks = jnp.stack([block for _ in range(size)])
+    blocks = lax.all_to_all(blocks, name, split_axis=0, concat_axis=0)
+    return jnp.concatenate(blocks, axis=along)
 
 
 def shifted(shard, axis, by):
@@ -71,7 +78,7 @@
         lax.all_gather(left_factor[0], "dp", axis=0, tiled=True),
         lax.all_gather(right_factor[0], "dp", axis=1, tiled=True),
     )
-    head = lax.all_gather(loss_grad, "pipe", axis=1, tiled=True)
+    head = gather_over(loss_grad, "pipe", 1)
     columns = block_column[0]
     inverse = inverse_of(columns)
     sections = lax.axis_size("pipe")

time: 1410 us -> 1420 us (level)
  waiting for transfers between devices: 729 us -> 652 us
  blocking collectives: 52.8 us -> 124 us
  starting transfers between devices: 96.1 us -> 116 us
    all_gather x1, blocking collectives: 29.2 us -> 102 us  [body(): lax.all_gather(left_factor[0], 'dp', axis=0, tiled=True)]
    all_gather x1 -> x0, waiting for transfers between devices: 41.7 us -> none  [body(): head = lax.all_gather(loss_grad, 'pipe', axis=1, tiled=True)]
    all_gather x1, waiting for transfers between devices: 28.8 us -> 0.01 us  [body(): lax.all_gather(weight_blocks[0], 'dp', axis=0, tiled=True)]
    all_to_all x0 -> x1, starting transfers between devices: none -> 16.3 us  [gather_over(): blocks = lax.all_to_all(blocks, name, split_axis=0, concat_axis=0)]
    ppermute x43, waiting for transfers between devices: 470 us -> 455 us  [shifted(): return lax.ppermute(shard, axis, pairs)]
    unnamed x7 -> x6, waiting for transfers between devices: 120 us -> 129 us
    while x87 -> x86, local copies, waits for them, and re-layouts: 34.3 us -> 30 us
    another operation x128 -> x129, local copies, waits for them, and re-layouts: 65.9 us -> 67.9 us
  transfers between devices with their start and end apart: 48 -> 48, of which waited for: 47 -> 45; matrix products, arithmetic and copies ran while one was open for 16% -> 16% of each run, Pallas kernels for 0% -> 0%
where the time goes in v1:
time: 1420 us
  waiting for transfers between devices  652 us (46%)
  other arithmetic  236 us (17%)
  local copies, waits for them, and re-layouts  156 us (11%)
  blocking collectives  124 us (9%)
  matrix products  118 us (8%)
  starting transfers between devices  116 us (8%)
    ppermute x43, waiting for transfers between devices, shifted(): return lax.ppermute(shard, axis, pairs)  455 us
    dynamic_update_slice x129, other arithmetic, replace_rows(): lax.dynamic_update_slice_in_dim(buffer, jnp.where(active, fresh, older),...  203 us
    unnamed x6, waiting for transfers between devices  129 us
    all_gather x1, blocking collectives, body(): lax.all_gather(left_factor[0], 'dp', axis=0, tiled=True)  102 us
    ppermute x43, starting transfers between devices, shifted(): return lax.ppermute(shard, axis, pairs)  99.8 us
    reduce_scatter x1, waiting for transfers between devices, body(): lax.psum_scatter(grad_blocks.astype(jnp.bfloat16), 'dp', scatter_dimensio...  67.9 us
    another operation x128, local copies, waits for them, and re-layouts  65 us
    while x86, local copies, waits for them, and re-layouts  30 us
  transfers between devices with their start and end apart: 48, of which 45 were waited for; matrix products, arithmetic and copies ran while one was open for 16% of the time, Pallas kernels for 0%

profile of v1, /device:TPU:8, one launch (start us, length us, event | category | flops | bytes accessed | tf_op | source)
XLA Modules:
  0.0 1417.4 jit_solution(12830151404134178841)
XLA Ops:
  7.2 2.9 stack.2
  10.1 16.3 %all-to-all-start = ((bf16[32,192,192]{2,1,0:T(8,128)(2,1)}), bf16[32,192,192]{2,1,0:T(8,128)(2,1)}, u32[]{:S(2)}, u32[]{:S(2)}) async-start(bf16[32,192,192]{2,1,0:T(8,128)(2,1)} %stack.2), calls=%async_computation | async-start | bytes 6291456 | tf_op jit(solution)/shard_map/all_to_all | solution.py:11
  31.2 102.1 %all-gather.1 = bf16[1,6144,64]{2,1,0:T(8,128)(2,1)S(1)} all-gather(bf16[1,384,64]{2,1,0:T(8,128)(2,1)S(1)} %copy.52), channel_id=3, replica_groups=mesh['pipe'=32,'dp'=16] {'dp'}, dimensions={1}, use_global_device_ids=true | all-gather | bytes 835584 | tf_op jit(solution)/shard_map/all_gather | solution.py:78
  133.3 22.1 %all-gather.2 = bf16[1,64,6144]{2,1,0:T(8,128)(2,1)} all-gather(bf16[1,64,384]{2,1,0:T(8,128)(2,1)S(1)} %copy-done.11), channel_id=4, replica_groups=mesh['pipe'=32,'dp'=16] {'dp'}, dimensions={2}, use_global_device_ids=true | all-gather | bytes 835584 | tf_op jit(solution)/shard_map/all_gather | solution.py:79
  155.4 5.3 copy.50
  160.8 6.2 reshape.96
  166.9 3.3 broadcast_select_fusion
  175.9 1022.5 %while.23 = (s32[]{:T(128)}, bf16[16,6144]{1,0:T(8,128)(2,1)}, bf16[192,6144]{1,0:T(8,128)(2,1)}, bf16[192,48,128]{2,0,1:T(8,128)(2,1)}, bf16[192,64]{1,0:T(8,12...) while((s32[]{:T(128)}, bf16[16,6144]{1,0:T(8,128)(2,1)}, ...), condition=%wide.region_5.6_spmd, body=%wide.region_2.5_spmd.sunk | while | flops 102833008 | bytes 20126928 | solution.py:136
  177.9 3.7 collective-permute-start
  189.8 3.7 collective-permute-start
  202.0 2.5 collective-permute-start
  231.1 2.3 collective-permute-done
  242.7 2.4 collective-permute-done
  254.4 2.4 collective-permute-done
  266.0 2.4 collective-permute-done
  277.7 4.7 collective-permute-done
  291.7 9.8 collective-permute-done
  310.8 6.4 collective-permute-done
  326.4 5.8 collective-permute-done
  341.4 5.3 collective-permute-done
  356.0 4.2 collective-permute-done
  369.5 3.2 collective-permute-done
  382.0 2.9 collective-permute-done
  394.2 6.4 collective-permute-done
  409.9 5.4 collective-permute-done
  424.5 3.9 collective-permute-done
  437.7 4.3 collective-permute-done
  451.3 3.9 collective-permute-done
  464.4 3.4 collective-permute-done
  477.0 4.3 collective-permute-done
  490.6 5.5 collective-permute-done
  505.4 8.3 collective-permute-done
  522.9 5.9 collective-permute-done
  538.1 4.8 collective-permute-done
  556.0 3.3 collective-permute-start
  575.3 270.2 %collective-permute-done = bf16[16,6144]{1,0:T(8,128)(2,1)S(1)} collective-permute-done((bf16[16,6144]{1,0:T(8,128)(2,1)}, bf16[16,6144]{1,0:T(8,128)(2,1)S(1)}, u32[]{:S(2)}, u32[]{:S(2)}) %collective-permute-start) | collective-permute-done | bytes 196640 | tf_op jit(solution)/shard_map/while/body/eval_jaxpr/ppermute | solution.py:18
  846.1 14.4 %conditional.2 = (bf16[16,6144]{1,0:T(8,128)(2,1)}, bf16[16,48,128]{2,0,1:T(8,128)(2,1)}, bf16[16,64]{1,0:T(8,128)(2,1)S(1)}, bf16[16,64]{1,0:T(8,128)(2,1)}) conditional(s32[]{:T(128)} %convert_element_type.80, () %tuple.64, (pred[]{:T(512)}, bf16[192,6144]{1,0:T(8,128)(2,1)}, s32[]{:T(128)}, bf16[16,6144]{1,0:T(8,128)(2,1)}, s32[48]{0:T(128)}, ...), branch_computations={%region_3.3_spmd, %region_4.4_spmd} | conditional | flops 102634336 | bytes 17349906 | solution.py:123
  867.3 10.2 collective-permute-done
  878.2 14.4 %conditional.2 = (bf16[16,6144]{1,0:T(8,128)(2,1)}, bf16[16,48,128]{2,0,1:T(8,128)(2,1)}, bf16[16,64]{1,0:T(8,128)(2,1)S(1)}, bf16[16,64]{1,0:T(8,128)(2,1)}) conditional(s32[]{:T(128)} %convert_element_type.80, () %tuple.64, (pred[]{:T(512)}, bf16[192,6144]{1,0:T(8,128)(2,1)}, s32[]{:T(128)}, bf16[16,6144]{1,0:T(8,128)(2,1)}, s32[48]{0:T(128)}, ...), branch_computations={%region_3.3_spmd, %region_4.4_spmd} | conditional | flops 102634336 | bytes 17349906 | solution.py:123
  899.4 6.8 collective-permute-done
  906.8 14.4 %conditional.2 = (bf16[16,6144]{1,0:T(8,128)(2,1)}, bf16[16,48,128]{2,0,1:T(8,128)(2,1)}, bf16[16,64]{1,0:T(8,128)(2,1)S(1)}, bf16[16,64]{1,0:T(8,128)(2,1)}) conditional(s32[]{:T(128)} %convert_element_type.80, () %tuple.64, (pred[]{:T(512)}, bf16[192,6144]{1,0:T(8,128)(2,1)}, s32[]{:T(128)}, bf16[16,6144]{1,0:T(8,128)(2,1)}, s32[48]{0:T(128)}, ...), branch_computations={%region_3.3_spmd, %region_4.4_spmd} | conditional | flops 102634336 | bytes 17349906 | solution.py:123
  928.0 6.1 collective-permute-done
  934.8 14.4 %conditional.2 = (bf16[16,6144]{1,0:T(8,128)(2,1)}, bf16[16,48,128]{2,0,1:T(8,128)(2,1)}, bf16[16,64]{1,0:T(8,128)(2,1)S(1)}, bf16[16,64]{1,0:T(8,128)(2,1)}) conditional(s32[]{:T(128)} %convert_element_type.80, () %tuple.64, (pred[]{:T(512)}, bf16[192,6144]{1,0:T(8,128)(2,1)}, s32[]{:T(128)}, bf16[16,6144]{1,0:T(8,128)(2,1)}, s32[48]{0:T(128)}, ...), branch_computations={%region_3.3_spmd, %region_4.4_spmd} | conditional | flops 102634336 | bytes 17349906 | solution.py:123
  956.0 5.4 collective-permute-done
  962.1 14.4 %conditional.2 = (bf16[16,6144]{1,0:T(8,128)(2,1)}, bf16[16,48,128]{2,0,1:T(8,128)(2,1)}, bf16[16,64]{1,0:T(8,128)(2,1)S(1)}, bf16[16,64]{1,0:T(8,128)(2,1)}) conditional(s32[]{:T(128)} %convert_element_type.80, () %tuple.64, (pred[]{:T(512)}, bf16[192,6144]{1,0:T(8,128)(2,1)}, s32[]{:T(128)}, bf16[16,6144]{1,0:T(8,128)(2,1)}, s32[48]{0:T(128)}, ...), branch_computations={%region_3.3_spmd, %region_4.4_spmd} | conditional | flops 102634336 | bytes 17349906 | solution.py:123
  983.2 4.2 collective-permute-done
  988.1 14.4 %conditional.2 = (bf16[16,6144]{1,0:T(8,128)(2,1)}, bf16[16,48,128]{2,0,1:T(8,128)(2,1)}, bf16[16,64]{1,0:T(8,128)(2,1)S(1)}, bf16[16,64]{1,0:T(8,128)(2,1)}) conditional(s32[]{:T(128)} %convert_element_type.80, () %tuple.64, (pred[]{:T(512)}, bf16[192,6144]{1,0:T(8,128)(2,1)}, s32[]{:T(128)}, bf16[16,6144]{1,0:T(8,128)(2,1)}, s32[48]{0:T(128)}, ...), branch_computations={%region_3.3_spmd, %region_4.4_spmd} | conditional | flops 102634336 | bytes 17349906 | solution.py:123
  1009.3 4.7 collective-permute-done
  1014.6 14.4 %conditional.2 = (bf16[16,6144]{1,0:T(8,128)(2,1)}, bf16[16,48,128]{2,0,1:T(8,128)(2,1)}, bf16[16,64]{1,0:T(8,128)(2,1)S(1)}, bf16[16,64]{1,0:T(8,128)(2,1)}) conditional(s32[]{:T(128)} %convert_element_type.80, () %tuple.64, (pred[]{:T(512)}, bf16[192,6144]{1,0:T(8,128)(2,1)}, s32[]{:T(128)}, bf16[16,6144]{1,0:T(8,128)(2,1)}, s32[48]{0:T(128)}, ...), branch_computations={%region_3.3_spmd, %region_4.4_spmd} | conditional | flops 102634336 | bytes 17349906 | solution.py:123
  1035.8 7.6 collective-permute-done
  1044.1 14.4 %conditional.2 = (bf16[16,6144]{1,0:T(8,128)(2,1)}, bf16[16,48,128]{2,0,1:T(8,128)(2,1)}, bf16[16,64]{1,0:T(8,128)(2,1)S(1)}, bf16[16,64]{1,0:T(8,128)(2,1)}) conditional(s32[]{:T(128)} %convert_element_type.80, () %tuple.64, (pred[]{:T(512)}, bf16[192,6144]{1,0:T(8,128)(2,1)}, s32[]{:T(128)}, bf16[16,6144]{1,0:T(8,128)(2,1)}, s32[48]{0:T(128)}, ...), branch_computations={%region_3.3_spmd, %region_4.4_spmd} | conditional | flops 102634336 | bytes 17349906 | solution.py:123
  1065.2 7.0 collective-permute-done
  1073.0 14.4 %conditional.2 = (bf16[16,6144]{1,0:T(8,128)(2,1)}, bf16[16,48,128]{2,0,1:T(8,128)(2,1)}, bf16[16,64]{1,0:T(8,128)(2,1)S(1)}, bf16[16,64]{1,0:T(8,128)(2,1)}) conditional(s32[]{:T(128)} %convert_element_type.80, () %tuple.64, (pred[]{:T(512)}, bf16[192,6144]{1,0:T(8,128)(2,1)}, s32[]{:T(128)}, bf16[16,6144]{1,0:T(8,128)(2,1)}, s32[48]{0:T(128)}, ...), branch_computations={%region_3.3_spmd, %region_4.4_spmd} | conditional | flops 102634336 | bytes 17349906 | solution.py:123
  1094.1 5.5 collective-permute-done
  1100.4 14.4 %conditional.2 = (bf16[16,6144]{1,0:T(8,128)(2,1)}, bf16[16,48,128]{2,0,1:T(8,128)(2,1)}, bf16[16,64]{1,0:T(8,128)(2,1)S(1)}, bf16[16,64]{1,0:T(8,128)(2,1)}) conditional(s32[]{:T(128)} %convert_element_type.80, () %tuple.64, (pred[]{:T(512)}, bf16[192,6144]{1,0:T(8,128)(2,1)}, s32[]{:T(128)}, bf16[16,6144]{1,0:T(8,128)(2,1)}, s32[48]{0:T(128)}, ...), branch_computations={%region_3.3_spmd, %region_4.4_spmd} | conditional | flops 102634336 | bytes 17349906 | solution.py:123
  1121.5 5.3 collective-permute-done
  1127.6 14.4 %conditional.2 = (bf16[16,6144]{1,0:T(8,128)(2,1)}, bf16[16,48,128]{2,0,1:T(8,128)(2,1)}, bf16[16,64]{1,0:T(8,128)(2,1)S(1)}, bf16[16,64]{1,0:T(8,128)(2,1)}) conditional(s32[]{:T(128)} %convert_element_type.80, () %tuple.64, (pred[]{:T(512)}, bf16[192,6144]{1,0:T(8,128)(2,1)}, s32[]{:T(128)}, bf16[16,6144]{1,0:T(8,128)(2,1)}, s32[48]{0:T(128)}, ...), branch_computations={%region_3.3_spmd, %region_4.4_spmd} | conditional | flops 102634336 | bytes 17349906 | solution.py:123
  1148.7 4.8 collective-permute-done
  1154.2 14.2 %conditional.2 = (bf16[16,6144]{1,0:T(8,128)(2,1)}, bf16[16,48,128]{2,0,1:T(8,128)(2,1)}, bf16[16,64]{1,0:T(8,128)(2,1)S(1)}, bf16[16,64]{1,0:T(8,128)(2,1)}) conditional(s32[]{:T(128)} %convert_element_type.80, () %tuple.64, (pred[]{:T(512)}, bf16[192,6144]{1,0:T(8,128)(2,1)}, s32[]{:T(128)}, bf16[16,6144]{1,0:T(8,128)(2,1)}, s32[48]{0:T(128)}, ...), branch_computations={%region_3.3_spmd, %region_4.4_spmd} | conditional | flops 102634336 | bytes 17349906 | solution.py:123
  1178.9 14.2 %collective-permute-start = (bf16[16,6144]{1,0:T(8,128)(2,1)}, bf16[16,6144]{1,0:T(8,128)(2,1)S(1)}, u32[]{:S(2)}, u32[]{:S(2)}) collective-permute-start(bf16[16,6144]{1,0:T(8,128)(2,1)} %get-tuple-element.571), channel_id=1, source_target_pairs={{16,0},{32,16},{48,32},{64,48},{80,64},{96,80},{112,96},{128,112},... | collective-permute-start | bytes 589832 | tf_op jit(solution)/shard_map/while/body/eval_jaxpr/ppermute | solution.py:18
  1207.9 2.3 fusion.17
  1210.2 59.9 %reduce-scatter.12.cloned.1.call-done = bf16[384,64]{1,0:T(8,128)(2,1)} async-done(((bf16[6144,64]{1,0:T(8,128)(2,1)}), bf16[384,64]{1,0:T(8,128)(2,1)}) %reduce-scatter.12.cloned.1.call-update) | async-done | bytes 49168
  1271.6 68.0 %reduce-scatter.10.cloned.1.call-done = bf16[384,64]{1,0:T(8,128)(2,1)} async-done(((bf16[6144,64]{1,0:T(8,128)(2,1)}), bf16[384,64]{1,0:T(8,128)(2,1)}) %reduce-scatter.10.cloned.1.call-update) | async-done | bytes 49168
  1341.3 67.9 %reduce-scatter.8.cloned.1.call-done = bf16[3,128,128]{1,2,0:T(8,128)(2,1)} async-done(((bf16[48,128,128]{1,2,0:T(8,128)(2,1)}), bf16[3,128,128]{1,2,0:T(8,128)(2,1)}) %reduce-scatter.8.cloned.1.call-update) | async-done | bytes 98320 | tf_op jit(solution)/shard_map/reduce_scatter | solution.py:142
  (790 shorter events, 633.9 us)
Async XLA Ops:
  10.1 17.2 %copy-start.12 = (bf16[1,384,64]{1,2,0:T(8,128)(2,1)S(1)}, bf16[1,384,64]{1,2,0:T(8,128)(2,1)}, u32[]{:S(2)}) copy-start(bf16[1,384,64]{1,2,0:T(8,128)(2,1)} %param.14) | copy-start | bytes 147460
  10.1 18.5 %copy-start.14 = (s32[1,12]{1,0:T(1,128)S(1)}, s32[1,12]{1,0:T(1,128)}, u32[]{:S(2)}) copy-start(s32[1,12]{1,0:T(1,128)} %param.17) | copy-start | bytes 148
  10.1 123.2 %copy-start.11 = (bf16[1,64,384]{2,1,0:T(8,128)(2,1)S(1)}, bf16[1,64,384]{2,1,0:T(8,128)(2,1)}, u32[]{:S(2)}) copy-start(bf16[1,64,384]{2,1,0:T(8,128)(2,1)} %param.15) | copy-start | bytes 147460
  10.1 145.3 %all-to-all-start = ((bf16[32,192,192]{2,1,0:T(8,128)(2,1)}), bf16[32,192,192]{2,1,0:T(8,128)(2,1)}, u32[]{:S(2)}, u32[]{:S(2)}) async-start(bf16[32,192,192]{2,1,0:T(8,128)(2,1)} %stack.2), calls=%async_computation | async-start | bytes 6291456 | tf_op jit(solution)/shard_map/all_to_all | solution.py:11
  26.5 143.8 %all-gather.5.cloned.1.call-start = ((), (), s32[]{:S(2)}) async-start(), calls=%async_computation.5 | async-start | bytes 1671168 | tf_op jit(solution)/shard_map/all_gather | solution.py:77
  27.2 1242.8 %reduce-scatter.12.cloned.1.call-start = ((), (), s32[]{:S(2)}) async-start(), calls=%async_computation.7 | async-start | bytes 1671168
  170.3 5.6 copy-start
  177.9 9.2 collective-permute-start
  189.8 9.5 collective-permute-start
  202.0 8.7 collective-permute-start
  213.4 8.4 collective-permute-start
  224.5 8.9 collective-permute-start
  236.1 9.0 collective-permute-start
  247.8 9.0 collective-permute-start
  259.4 9.0 collective-permute-start
  271.1 11.3 collective-permute-start
  285.1 16.4 %collective-permute-start = (bf16[16,6144]{1,0:T(8,128)(2,1)}, bf16[16,6144]{1,0:T(8,128)(2,1)S(1)}, u32[]{:S(2)}, u32[]{:S(2)}) collective-permute-start(bf16[16,6144]{1,0:T(8,128)(2,1)} %get-tuple-element.571), channel_id=1, source_target_pairs={{16,0},{32,16},{48,32},{64,48},{80,64},{96,80},{112,96},{128,112},... | collective-permute-start | bytes 589832 | tf_op jit(solution)/shard_map/while/body/eval_jaxpr/ppermute | solution.py:18
  304.2 12.9 collective-permute-start
  319.8 12.4 collective-permute-start
  334.9 11.9 collective-permute-start
  349.4 10.8 collective-permute-start
  362.9 9.8 collective-permute-start
  375.4 9.5 collective-permute-start
  387.6 13.0 collective-permute-start
  403.3 12.0 collective-permute-start
  417.9 10.5 collective-permute-start
  431.1 10.9 collective-permute-start
  444.7 10.5 collective-permute-start
  457.8 10.0 collective-permute-start
  470.4 10.9 collective-permute-start
  484.0 12.1 collective-permute-start
  498.8 14.9 %collective-permute-start = (bf16[16,6144]{1,0:T(8,128)(2,1)}, bf16[16,6144]{1,0:T(8,128)(2,1)S(1)}, u32[]{:S(2)}, u32[]{:S(2)}) collective-permute-start(bf16[16,6144]{1,0:T(8,128)(2,1)} %get-tuple-element.571), channel_id=1, source_target_pairs={{16,0},{32,16},{48,32},{64,48},{80,64},{96,80},{112,96},{128,112},... | collective-permute-start | bytes 589832 | tf_op jit(solution)/shard_map/while/body/eval_jaxpr/ppermute | solution.py:18
  516.3 12.5 collective-permute-start
  531.5 11.4 collective-permute-start
  545.6 7.8 collective-permute-start
  556.0 10.0 collective-permute-start
  568.7 276.8 %collective-permute-start = (bf16[16,6144]{1,0:T(8,128)(2,1)}, bf16[16,6144]{1,0:T(8,128)(2,1)S(1)}, u32[]{:S(2)}, u32[]{:S(2)}) collective-permute-start(bf16[16,6144]{1,0:T(8,128)(2,1)} %get-tuple-element.571), channel_id=1, source_target_pairs={{16,0},{32,16},{48,32},{64,48},{80,64},{96,80},{112,96},{128,112},... | collective-permute-start | bytes 589832 | tf_op jit(solution)/shard_map/while/body/eval_jaxpr/ppermute | solution.py:18
  850.9 6.5 copy-start.8
  860.5 17.0 %collective-permute-start = (bf16[16,6144]{1,0:T(8,128)(2,1)}, bf16[16,6144]{1,0:T(8,128)(2,1)S(1)}, u32[]{:S(2)}, u32[]{:S(2)}) collective-permute-start(bf16[16,6144]{1,0:T(8,128)(2,1)} %get-tuple-element.571), channel_id=1, source_target_pairs={{16,0},{32,16},{48,32},{64,48},{80,64},{96,80},{112,96},{128,112},... | collective-permute-start | bytes 589832 | tf_op jit(solution)/shard_map/while/body/eval_jaxpr/ppermute | solution.py:18
  883.0 6.5 copy-start.8
  892.6 13.5 collective-permute-start
  911.6 6.5 copy-start.8
  921.2 12.9 collective-permute-start
  939.6 6.5 copy-start.8
  949.2 12.2 collective-permute-start
  966.9 6.5 copy-start.8
  976.5 10.9 collective-permute-start
  992.9 6.5 copy-start.8
  1002.5 11.4 collective-permute-start
  1019.4 6.5 copy-start.8
  1029.0 14.4 %collective-permute-start = (bf16[16,6144]{1,0:T(8,128)(2,1)}, bf16[16,6144]{1,0:T(8,128)(2,1)S(1)}, u32[]{:S(2)}, u32[]{:S(2)}) collective-permute-start(bf16[16,6144]{1,0:T(8,128)(2,1)} %get-tuple-element.571), channel_id=1, source_target_pairs={{16,0},{32,16},{48,32},{64,48},{80,64},{96,80},{112,96},{128,112},... | collective-permute-start | bytes 589832 | tf_op jit(solution)/shard_map/while/body/eval_jaxpr/ppermute | solution.py:18
  1048.9 6.5 copy-start.8
  1058.5 13.8 collective-permute-start
  1077.8 6.5 copy-start.8
  1087.4 12.3 collective-permute-start
  1105.1 6.5 copy-start.8
  1114.7 12.1 collective-permute-start
  1132.3 6.5 copy-start.8
  1141.9 11.6 collective-permute-start
  1158.9 6.4 copy-start.8
  1168.5 7.8 collective-permute-start
  1178.9 18.8 %collective-permute-start = (bf16[16,6144]{1,0:T(8,128)(2,1)}, bf16[16,6144]{1,0:T(8,128)(2,1)S(1)}, u32[]{:S(2)}, u32[]{:S(2)}) collective-permute-start(bf16[16,6144]{1,0:T(8,128)(2,1)} %get-tuple-element.571), channel_id=1, source_target_pairs={{16,0},{32,16},{48,32},{64,48},{80,64},{96,80},{112,96},{128,112},... | collective-permute-start | bytes 589832 | tf_op jit(solution)/shard_map/while/body/eval_jaxpr/ppermute | solution.py:18
  1203.3 136.4 %reduce-scatter.10.cloned.1.call-start = ((), (), s32[]{:S(2)}) async-start(), calls=%async_computation.6 | async-start | bytes 1671168
  1206.1 203.1 %reduce-scatter.8.cloned.1.call-start = ((), (), s32[]{:S(2)}) async-start(), calls=%async_computation.4 | async-start | bytes 1671168 | tf_op jit(solution)/shard_map/reduce_scatter | solution.py:142
  (107 other events, 180.4 us)
Sparse Core Ops, SparseCore 0:
  29.4 92.9 all-gather.4
  1203.4 66.5 reduce-scatter.11
  1272.9 66.7 reduce-scatter.9
  1342.4 66.7 reduce-scatter.7
